TPU v7x, 128 devices: a whole 4x4x4 slice. The times are simulated.
128 devices in a mesh: strip: 8 (over x, y_lo), along: 16 (over z, y_hi, core).
Axes of the slice: x: 4, y: 4 (y_hi: 2, y_lo: 2; y = y_hi * 2 + y_lo), z: 4, core: 2. Of those that a mesh axis runs over, the one named last changes fastest.
Arguments:
- images: float32 [512, 8192], P('strip', 'along'), may hold values from 0 to 255
- offsets: int32 [8, 16, 2], P('strip', 'along'), may hold values from 0 to 31
Outputs:
- matches: float32 [8, 512, 8192], P(None, 'strip', 'along')
All inputs are finite; a program needn't handle non-finite values.
Results may differ from a plain program's by a relative error of at most 0.000063.
Values sent between devices are 32-bit elements; how exact they have to be, the bound alone decides.
A program may use at most 64 MiB of HBM per device.

v0:
```python
import functools
import jax
import jax.numpy as jnp
from jax import lax
from jax.experimental import pallas as pl
from jax.experimental.pallas import tpu as pltpu
from jax.sharding import PartitionSpec as P

F32 = jnp.float32
BF16 = jnp.bfloat16
ROWS, COLS, GROUPS, SUB, LANES = 64, 512, 8, 8, 128
HALF = LANES // 2
RADIUS = 4
UNROLL = 16
SCALE = -4.0 * 1.4426950408889634


def lane_ids(shape):
    return lax.broadcasted_iota(jnp.int32, shape, len(shape) - 1)


def split3(x):
    hi = x.astype(BF16)
    rest = x - hi.astype(F32)
    mid = rest.astype(BF16)
    low = (rest - mid.astype(F32)).astype(BF16)
    return jnp.concatenate([hi, mid, low], axis=0)


def permuted(x, perm, transposed):
    n = x.shape[0]
    dims = (((1,), (1 if transposed else 0,)), ((), ()))
    out = lax.dot_general(split3(x), perm, dims, preferred_element_type=F32)
    return out[:n] + out[n : 2 * n] + out[2 * n :]


def fill_perm(perm_ref):
    for k in range(4):
        shape = (128, COLS)
        n = lax.broadcasted_iota(jnp.int32, shape, 1)
        c = lax.broadcasted_iota(jnp.int32, shape, 0) + 128 * k
        hit = c == 8 * (n & 63) + (n >> 6)
        perm_ref[pl.ds(128 * k, 128), :] = jnp.where(hit, 1.0, 0.0).astype(BF16)


def spread(x, perm):
    y = permuted(x, perm, False)
    low = lane_ids((x.shape[0], LANES)) < HALF
    out = []
    for k in range(4):
        v = y[:, LANES * k : LANES * (k + 1)]
        w = pltpu.roll(v, HALF, 1)
        out += [jnp.where(low, v, w), jnp.where(low, w, v)]
    return out


def row_box(x):
    shape = x[0].shape
    pos = lane_ids(shape) & (HALF - 1)
    first, last = pos == 0, pos == HALF - 1
    pre = [x[0]]
    for k in range(1, 8):
        pre.append(pre[-1] + x[k])
    suf = [None] * 8
    suf[7] = x[7]
    for k in range(6, 0, -1):
        suf[k] = suf[k + 1] + x[k]
    suf[0] = pre[7]
    out = []
    for j in range(4):
        out.append(jnp.where(first, 0.0, pltpu.roll(suf[j + 4], 1, 1)) + pre[j + 4])
    for j in range(4, 8):
        out.append(jnp.where(last, 0.0, pltpu.roll(pre[j - 4], LANES - 1, 1)) + suf[j - 4])
    return out


def guide_fields(g, perm, pad_ref, g_ref, a1_ref, a2_ref, i4_ref, mg_ref, inv_ref):
    gd = spread(g, perm)
    zero = jnp.zeros((SUB, LANES), F32)
    for j in range(8):
        g_ref[j] = gd[j]
        for n, field in enumerate((gd[j], gd[j] * gd[j])):
            at = 2 * j + n
            pad_ref[at, pl.ds(0, SUB), :] = zero
            pad_ref[at, pl.ds(SUB, ROWS), :] = field
            pad_ref[at, pl.ds(SUB + ROWS, SUB), :] = zero

    def tile(i, carry):
        base = pl.multiple_of(i * SUB, SUB)
        sums = []
        for at in range(16):
            total = pad_ref[at, pl.ds(base + SUB - RADIUS, SUB), :]
            for k in range(1, 2 * RADIUS + 1):
                total = total + pad_ref[at, pl.ds(base + SUB - RADIUS + k, SUB), :]
            sums.append(total)
        bg, bgg = row_box(sums[0::2]), row_box(sums[1::2])
        shape = (SUB, LANES)
        r = lax.broadcasted_iota(jnp.int32, shape, 0) + base
        nr = jnp.minimum(r + RADIUS, ROWS - 1) - jnp.maximum(r - RADIUS, 0) + 1
        l8 = 8 * (lane_ids(shape) & (HALF - 1))
        for j in range(8):
            c = l8 + j
            nc = jnp.minimum(c + RADIUS, COLS - 1) - jnp.maximum(c - RADIUS, 0) + 1
            inv = 1.0 / (nr * nc).astype(F32)
            mean = bg[j] * inv
            var = bgg[j] * inv - mean * mean
            a1 = (SCALE * inv) / (var + 50.0)
            here = pl.ds(base, SUB)
            a1_ref[j, here, :] = a1
            a2_ref[j, here, :] = a1 * mean
            i4_ref[j, here, :] = SCALE * inv
            mg_ref[j, here, :] = mean
            inv_ref[j, here, :] = inv
        return carry

    lax.fori_loop(0, ROWS // SUB, tile, 0)


def forward_table(f, shift, perm, z_ref):
    base = spread(pltpu.roll(f, COLS - shift, 1), perm)
    low = lane_ids((ROWS, LANES)) < HALF
    for e in range(8):
        one = pltpu.roll(base[e], LANES - 1, 1)
        two = pltpu.roll(one, LANES - 1, 1)
        z_ref[pl.ds(e, ROWS, stride=16), :] = jnp.where(low, base[e], one)
        z_ref[pl.ds(e + 8, ROWS, stride=16), :] = jnp.where(low, one, two)


def side_table(s, shift, perm, y_ref, pad_ref):
    base = spread(pltpu.roll(s, ROWS - shift, 0), perm)
    low = lane_ids((SUB, LANES)) < HALF
    for j in range(8):
        tiles = [base[j][SUB * k : SUB * (k + 1)] for k in range(8)]
        for k in range(9):
            y_ref[j, pl.ds(SUB * k, SUB), :] = jnp.where(low, tiles[k % 8], tiles[(k + 1) % 8])


def bcast(ref, j, r):
    return jnp.broadcast_to(ref[j, pl.ds(r, 1), :], (SUB, LANES))


def cost_pass(load, g_ref, hx_ref, hy_ref):
    def row(r, carry):
        xs, ys = [], []
        for j in range(8):
            g = bcast(g_ref, j, r)
            x = jnp.abs(g - load(r, j))
            xs.append(x)
            ys.append(g * x)
        for ref, vals in ((hx_ref, xs), (hy_ref, ys)):
            for j, v in enumerate(row_box(vals)):
                ref[j, r] = v
        return carry

    lax.fori_loop(0, ROWS, row, 0, unroll=UNROLL)


def coef_pass(hx_ref, hy_ref, wa_ref, wb_ref, a1_ref, a2_ref, i4_ref, mg_ref):
    def column(j, carry):
        def window(ref):
            total = ref[j, 0]
            for r in range(1, RADIUS):
                total = total + ref[j, r]
            return total

        p, q = window(hx_ref), window(hy_ref)
        olda, oldb = [], []
        wa = wb = None
        for r in range(ROWS + RADIUS):
            if r < ROWS:
                if r + RADIUS < ROWS:
                    if r > RADIUS:
                        p = p + (hx_ref[j, r + RADIUS] - hx_ref[j, r - RADIUS - 1])
                        q = q + (hy_ref[j, r + RADIUS] - hy_ref[j, r - RADIUS - 1])
                    else:
                        p = p + hx_ref[j, r + RADIUS]
                        q = q + hy_ref[j, r + RADIUS]
                else:
                    p = p - hx_ref[j, r - RADIUS - 1]
                    q = q - hy_ref[j, r - RADIUS - 1]
                ca = q * bcast(a1_ref, j, r) - p * bcast(a2_ref, j, r)
                cb = p * bcast(i4_ref, j, r) - ca * bcast(mg_ref, j, r)
                olda.append(ca)
                oldb.append(cb)
                if r == 0:
                    wa, wb = ca, cb
                elif r > 2 * RADIUS:
                    wa = wa + (ca - olda[r - 2 * RADIUS - 1])
                    wb = wb + (cb - oldb[r - 2 * RADIUS - 1])
                else:
                    wa, wb = wa + ca, wb + cb
            else:
                wa = wa - olda[r - 2 * RADIUS - 1]
                wb = wb - oldb[r - 2 * RADIUS - 1]
            if r >= RADIUS:
                wa_ref[j, r - RADIUS] = wa
                wb_ref[j, r - RADIUS] = wb
        return carry

    lax.fori_loop(0, 8, column, 0)


def score_pass(wa_ref, wb_ref, g_ref, inv_ref, sc_ref):
    def row(r, carry):
        ha = row_box([wa_ref[j, r] for j in range(8)])
        hb = row_box([wb_ref[j, r] for j in range(8)])
        for j in range(8):
            sc_ref[r, pl.ds(SUB * j, SUB), :] = (ha[j] * bcast(g_ref, j, r) + hb[j]) * bcast(inv_ref, j, r)
        return carry

    lax.fori_loop(0, ROWS, row, 0, unroll=UNROLL)


def softmax_pass(sc_ref, d_ref, c_ref):
    def row(r, carry):
        high = lane_ids((SUB, LANES)) >= HALF
        t = [sc_ref[r, pl.ds(s, SUB, stride=SUB), :] for s in range(8)]
        top = t[0]
        for s in range(1, 8):
            top = jnp.maximum(top, t[s])
        top = jnp.maximum(top, pltpu.roll(top, HALF, 1))
        total = lift = square = None
        for s in range(7, -1, -1):
            w = jnp.exp2(t[s] - top)
            total = w if total is None else total + w
            square = w * w if square is None else square + w * w
            if s:
                lift = total if lift is None else lift + total
        lift = lift + jnp.where(high, 8.0 * total, 0.0)
        total = total + pltpu.roll(total, HALF, 1)
        lift = lift + pltpu.roll(lift, HALF, 1)
        square = square + pltpu.roll(square, HALF, 1)
        unit = 1.0 / total
        d_ref[pl.ds(pl.multiple_of(r * SUB, SUB), SUB), :] = lift * unit
        c_ref[pl.ds(pl.multiple_of(r * SUB, SUB), SUB), :] = square * unit * unit
        return carry

    lax.fori_loop(0, ROWS, row, 0, unroll=UNROLL)


def gathered(ref, perm):
    low = lane_ids((ROWS, LANES)) < HALF
    parts = []
    for k in range(4):
        even = ref[pl.ds(2 * k, ROWS, stride=SUB), :]
        odd = ref[pl.ds(2 * k + 1, ROWS, stride=SUB), :]
        parts.append(jnp.where(low, even, odd))
    return permuted(jnp.concatenate(parts, axis=1), perm, True)


SCRATCH = dict(
    perm=((COLS, COLS), BF16), pad=((16, ROWS + 16, LANES), F32),
    g=((8, ROWS, LANES), F32), a1=((8, ROWS, LANES), F32), a2=((8, ROWS, LANES), F32),
    i4=((8, ROWS, LANES), F32), mg=((8, ROWS, LANES), F32), inv=((8, ROWS, LANES), F32),
    z=((16 * ROWS, LANES), F32), y=((8, ROWS + SUB, LANES), F32),
    hx=((8, ROWS, SUB, LANES), F32), hy=((8, ROWS, SUB, LANES), F32),
    wa=((8, ROWS, SUB, LANES), F32), wb=((8, ROWS, SUB, LANES), F32),
    sc=((ROWS, SUB * SUB, LANES), F32), d=((ROWS * SUB, LANES), F32), c=((ROWS * SUB, LANES), F32),
)


def levels(load, b):
    cost_pass(load, b["g"], b["hx"], b["hy"])
    coef_pass(b["hx"], b["hy"], b["wa"], b["wb"], b["a1"], b["a2"], b["i4"], b["mg"])
    score_pass(b["wa"], b["wb"], b["g"], b["inv"], b["sc"])
    softmax_pass(b["sc"], b["d"], b["c"])


def load_forward(b):
    return lambda r, j: b["z"][pl.ds(r * 16 + j, SUB), :]


def load_side(b):
    return lambda r, j: b["y"][j, pl.ds(r, SUB), :]
def kernel(t_ref, g_ref, f_ref, s_ref, o_ref, *bufs):
    b = dict(zip(SCRATCH, bufs))
    perm = b["perm"]
    fill_perm(perm)
    guide_fields(g_ref[...], perm[...], b["pad"], b["g"], b["a1"], b["a2"], b["i4"], b["mg"], b["inv"])
    forward_table(f_ref[...], t_ref[0], perm[...], b["z"])
    levels(load_forward(b), b)
    o_ref[0] = gathered(b["d"], perm[...])
    o_ref[1] = gathered(b["c"], perm[...])
    side_table(s_ref[...], t_ref[1], perm[...], b["y"], b["pad"])
    levels(load_side(b), b)
    o_ref[2] = gathered(b["d"], perm[...])
    o_ref[3] = gathered(b["c"], perm[...])

def maps(t, g, f, s):
    V = pl.BlockSpec(memory_space=pltpu.VMEM)
    return pl.pallas_call(kernel, out_shape=jax.ShapeDtypeStruct((4, ROWS, COLS), F32),
        in_specs=[pl.BlockSpec(memory_space=pltpu.SMEM), V, V, V], out_specs=V,
        scratch_shapes=[pltpu.VMEM(*v) for v in SCRATCH.values()],
        compiler_params=pltpu.CompilerParams(vmem_limit_bytes=60 << 20))(t, g, f, s)


def from_behind(value, axis, steps):
    count = lax.axis_size(axis)
    leading, last = (max(0, -steps), min(count, count - steps))
    return lax.ppermute(value, axis, [(source, source + steps) for source in range(leading, last)])


def per_device(images, offsets):
    forward = from_behind(images, "along", -1)
    side = from_behind(images, "strip", -1)
    own = maps(offsets.reshape(2), images, forward, side)
    fwd_back = from_behind(own[0:2], "along", 1)
    side_back = from_behind(own[2:4], "strip", 1)
    return jnp.concatenate([own[0:2], fwd_back, own[2:4], side_back], axis=0)


def solution(mesh):
    placed = (P("strip", "along"), P("strip", "along", None))
    return jax.shard_map(
        per_device, mesh=mesh, in_specs=placed, out_specs=P(None, "strip", "along"), check_vma=False
    )
```

profile of v0, /device:TPU:108, one launch (start us, length us, event | category | flops | bytes accessed | tf_op | source)
XLA Modules:
  0.0 44.9 jit_solution(9954975810769180182)
XLA Ops:
  0.0 3.5 %collective-permute-start = (f32[64,512]{1,0:T(8,128)}, f32[64,512]{1,0:T(8,128)S(1)}, u32[]{:S(2)}, u32[]{:S(2)}) collective-permute-start(f32[64,512]{1,0:T(8,128)} %g_ref.1), channel_id=1, source_target_pairs={{1,0},{2,1},{3,2},{4,3},{5,4},{6,5},{7,6},{8,7},{9,8},{10,9},{11,1... | collective-permute-start | bytes 393224 | tf_op jit(solution)/shard_map/ppermute | solution.py:300
  3.5 3.3 %collective-permute-start.1 = (f32[64,512]{1,0:T(8,128)}, f32[64,512]{1,0:T(8,128)S(1)}, u32[]{:S(2)}, u32[]{:S(2)}) collective-permute-start(f32[64,512]{1,0:T(8,128)} %g_ref.1), channel_id=1, source_target_pairs={{16,0},{32,16},{48,32},{64,48},{80,64},{96,80},{112,96},{17,1},{33... | collective-permute-start | bytes 393224 | tf_op jit(solution)/shard_map/ppermute | solution.py:300
  6.7 0.6 %collective-permute-done.f_ref = f32[64,512]{1,0:T(8,128)S(1)} collective-permute-done((f32[64,512]{1,0:T(8,128)}, f32[64,512]{1,0:T(8,128)S(1)}, u32[]{:S(2)}, u32[]{:S(2)}) %collective-permute-start) | collective-permute-done | bytes 131104 | tf_op jit(solution)/shard_map/ppermute | solution.py:300
  7.3 0.0 copy-start
  7.3 4.1 %collective-permute-done.1.s_ref = f32[64,512]{1,0:T(8,128)S(1)} collective-permute-done((f32[64,512]{1,0:T(8,128)}, f32[64,512]{1,0:T(8,128)S(1)}, u32[]{:S(2)}, u32[]{:S(2)}) %collective-permute-start.1) | collective-permute-done | bytes 131104 | tf_op jit(solution)/shard_map/ppermute | solution.py:300
  11.4 0.0 copy-start.1
  11.5 0.0 copy-done
  11.5 0.6 %copy-done.1 = f32[64,512]{1,0:T(8,128)} copy-done((f32[64,512]{1,0:T(8,128)}, f32[64,512]{1,0:T(8,128)S(1)}, u32[]{:S(2)}) %copy-start.1) | copy-done | bytes 131096
  12.1 14.9 %shard_map.28 = f32[4,64,512]{2,1,0:T(8,128)} custom-call(s32[2]{0:T(128)} %bitcast.1, f32[64,512]{1,0:T(8,128)} %g_ref.1, f32[64,512]{1,0:T(8,128)} %copy-done, f32[64,512]{1,0:T(8,128)} %copy-done.1), custom_call_target="tpu_custom_call" | custom-call | tf_op jit(solution)/shard_map/pallas_call | solution.py:291
  27.0 1.1 %fusion = (f32[2,64,512]{2,1,0:T(8,128)S(1)}, f32[2,64,512]{2,1,0:T(8,128)S(1)}) fusion(f32[4,64,512]{2,1,0:T(8,128)} %shard_map.28), kind=kLoop, calls=%fused_computation.1 | loop fusion | bytes 1048576 | tf_op jit(solution)/shard_map/slice | solution.py:309
  28.1 1.9 %collective-permute-start.2 = (f32[2,64,512]{2,1,0:T(8,128)S(1)}, f32[2,64,512]{2,1,0:T(8,128)S(1)}, u32[]{:S(2)}, u32[]{:S(2)}) collective-permute-start(f32[2,64,512]{2,1,0:T(8,128)S(1)} %get-tuple-element.5), channel_id=1, source_target_pairs={{0,1},{1,2},{2,3},{3,4},{4,5},{5,6},{6,7},{7,8},{8,9},{9,10},{10,1... | collective-permute-start | bytes 786440 | tf_op jit(solution)/shard_map/ppermute | solution.py:300
  30.0 3.0 %collective-permute-start.3 = (f32[2,64,512]{2,1,0:T(8,128)S(1)}, f32[2,64,512]{2,1,0:T(8,128)S(1)}, u32[]{:S(2)}, u32[]{:S(2)}) collective-permute-start(f32[2,64,512]{2,1,0:T(8,128)S(1)} %get-tuple-element.6), channel_id=1, source_target_pairs={{0,16},{16,32},{32,48},{48,64},{64,80},{80,96},{96,112},{1,17},{17... | collective-permute-start | bytes 786440 | tf_op jit(solution)/shard_map/ppermute | solution.py:300
  33.0 10.8 %collective-permute-done.2 = f32[2,64,512]{2,1,0:T(8,128)S(1)} collective-permute-done((f32[2,64,512]{2,1,0:T(8,128)S(1)}, f32[2,64,512]{2,1,0:T(8,128)S(1)}, u32[]{:S(2)}, u32[]{:S(2)}) %collective-permute-start.2) | collective-permute-done | bytes 262176 | tf_op jit(solution)/shard_map/ppermute | solution.py:300
  43.8 0.0 collective-permute-done.3
  43.8 1.0 %pad_maximum_fusion = f32[8,64,512]{2,1,0:T(8,128)} fusion(f32[2,64,512]{2,1,0:T(8,128)S(1)} %collective-permute-done.3, f32[2,64,512]{2,1,0:T(8,128)S(1)} %get-tuple-element.6, f32[2,64,512]{2,1,0:T(8,128)S(1)} %collective-permute-done.2, f32[2,64,512]{2,1,0:T(8,128)S(1)} %get-tuple-element.5), kind=kLoop, calls=%fused_computation | loop fusion | flops 786432 | bytes 2097152 | tf_op jit(solution)/shard_map/concatenate | solution.py:309
Async XLA Ops:
  0.0 7.3 %collective-permute-start = (f32[64,512]{1,0:T(8,128)}, f32[64,512]{1,0:T(8,128)S(1)}, u32[]{:S(2)}, u32[]{:S(2)}) collective-permute-start(f32[64,512]{1,0:T(8,128)} %g_ref.1), channel_id=1, source_target_pairs={{1,0},{2,1},{3,2},{4,3},{5,4},{6,5},{7,6},{8,7},{9,8},{10,9},{11,1... | collective-permute-start | bytes 393224 | tf_op jit(solution)/shard_map/ppermute | solution.py:300
  3.5 8.0 %collective-permute-start.1 = (f32[64,512]{1,0:T(8,128)}, f32[64,512]{1,0:T(8,128)S(1)}, u32[]{:S(2)}, u32[]{:S(2)}) collective-permute-start(f32[64,512]{1,0:T(8,128)} %g_ref.1), channel_id=1, source_target_pairs={{16,0},{32,16},{48,32},{64,48},{80,64},{96,80},{112,96},{17,1},{33... | collective-permute-start | bytes 393224 | tf_op jit(solution)/shard_map/ppermute | solution.py:300
  7.3 4.1 %copy-start = (f32[64,512]{1,0:T(8,128)}, f32[64,512]{1,0:T(8,128)S(1)}, u32[]{:S(2)}) copy-start(f32[64,512]{1,0:T(8,128)S(1)} %collective-permute-done.f_ref) | copy-start | bytes 393220
  11.4 0.7 %copy-start.1 = (f32[64,512]{1,0:T(8,128)}, f32[64,512]{1,0:T(8,128)S(1)}, u32[]{:S(2)}) copy-start(f32[64,512]{1,0:T(8,128)S(1)} %collective-permute-done.1.s_ref) | copy-start | bytes 393220
  28.1 15.7 %collective-permute-start.2 = (f32[2,64,512]{2,1,0:T(8,128)S(1)}, f32[2,64,512]{2,1,0:T(8,128)S(1)}, u32[]{:S(2)}, u32[]{:S(2)}) collective-permute-start(f32[2,64,512]{2,1,0:T(8,128)S(1)} %get-tuple-element.5), channel_id=1, source_target_pairs={{0,1},{1,2},{2,3},{3,4},{4,5},{5,6},{6,7},{7,8},{8,9},{9,10},{10,1... | collective-permute-start | bytes 786440 | tf_op jit(solution)/shard_map/ppermute | solution.py:300
  30.0 13.8 %collective-permute-start.3 = (f32[2,64,512]{2,1,0:T(8,128)S(1)}, f32[2,64,512]{2,1,0:T(8,128)S(1)}, u32[]{:S(2)}, u32[]{:S(2)}) collective-permute-start(f32[2,64,512]{2,1,0:T(8,128)S(1)} %get-tuple-element.6), channel_id=1, source_target_pairs={{0,16},{16,32},{32,48},{48,64},{64,80},{80,96},{96,112},{1,17},{17... | collective-permute-start | bytes 786440 | tf_op jit(solution)/shard_map/ppermute | solution.py:300
where the time goes:
time: 45.1 us; the launch traced here: 44.9 us
  waiting for transfers between devices  15.5 us (34%)
  Pallas kernels  14.9 us (33%)
  starting transfers between devices  11.6 us (26%)
  local copies, waits for them, and re-layouts  1.71 us (4%)
  other arithmetic  1.04 us (2%)
    ppermute x4, waiting for transfers between devices, from_behind(): lax.ppermute(value, axis, [(source, source + steps) for source in range(l...  15.5 us
    pallas_call x1, Pallas kernels, maps(): pl.pallas_call(kernel, out_shape=jax.ShapeDtypeStruct((4, ROWS, COLS), F3...  14.9 us
    ppermute x4, starting transfers between devices, from_behind(): lax.ppermute(value, axis, [(source, source + steps) for source in range(l...  11.6 us
    slice x1, local copies, waits for them, and re-layouts, per_device(): return jnp.concatenate([own[0:2], fwd_back, own[2:4], side_back], axis=0)  1.06 us
    concatenate x1, other arithmetic, per_device(): return jnp.concatenate([own[0:2], fwd_back, own[2:4], side_back], axis=0)  1.04 us
  transfers between devices with their start and end apart: 4, of which 3 were waited for; matrix products, arithmetic and copies ran while one was open for 0% of the time, Pallas kernels for 0%

commit v1 on v0

--- a/solution.py
+++ b/solution.py
@@ -200,19 +200,21 @@
     lax.fori_loop(0, 8, column, 0)
 
 
-def score_pass(wa_ref, wb_ref, g_ref, inv_ref, sc_ref):
-    def row(r, carry):
+def score_pass(start, rows, wa_ref, wb_ref, g_ref, inv_ref, sc_ref):
+    def row(i, carry):
+        r = start + i
         ha = row_box([wa_ref[j, r] for j in range(8)])
         hb = row_box([wb_ref[j, r] for j in range(8)])
         for j in range(8):
             sc_ref[r, pl.ds(SUB * j, SUB), :] = (ha[j] * bcast(g_ref, j, r) + hb[j]) * bcast(inv_ref, j, r)
         return carry
 
-    lax.fori_loop(0, ROWS, row, 0, unroll=UNROLL)
-
-
-def softmax_pass(sc_ref, d_ref, c_ref):
-    def row(r, carry):
+    lax.fori_loop(0, rows, row, 0, unroll=min(UNROLL, rows))
+
+
+def softmax_pass(start, rows, sc_ref, d_ref, c_ref):
+    def row(i, carry):
+        r = start + i
         high = lane_ids((SUB, LANES)) >= HALF
         t = [sc_ref[r, pl.ds(s, SUB, stride=SUB), :] for s in range(8)]
         top = t[0]
@@ -235,17 +237,20 @@
         c_ref[pl.ds(pl.multiple_of(r * SUB, SUB), SUB), :] = square * unit * unit
         return carry
 
-    lax.fori_loop(0, ROWS, row, 0, unroll=UNROLL)
-
-
-def gathered(ref, perm):
-    low = lane_ids((ROWS, LANES)) < HALF
-    parts = []
-    for k in range(4):
-        even = ref[pl.ds(2 * k, ROWS, stride=SUB), :]
-        odd = ref[pl.ds(2 * k + 1, ROWS, stride=SUB), :]
-        parts.append(jnp.where(low, even, odd))
-    return permuted(jnp.concatenate(parts, axis=1), perm, True)
+    lax.fori_loop(0, rows, row, 0, unroll=min(UNROLL, rows))
+
+
+def gathered(start, rows, refs, perm):
+    low = lane_ids((rows, LANES)) < HALF
+    stacked = []
+    for ref in refs:
+        parts = []
+        for k in range(4):
+            even = ref[pl.ds(SUB * start + 2 * k, rows, stride=SUB), :]
+            odd = ref[pl.ds(SUB * start + 2 * k + 1, rows, stride=SUB), :]
+            parts.append(jnp.where(low, even, odd))
+        stacked.append(jnp.concatenate(parts, axis=1))
+    return permuted(jnp.concatenate(stacked, axis=0), perm, True)
 
 
 SCRATCH = dict(
@@ -259,54 +264,151 @@
 )
 
 
-def levels(load, b):
-    cost_pass(load, b["g"], b["hx"], b["hy"])
-    coef_pass(b["hx"], b["hy"], b["wa"], b["wb"], b["a1"], b["a2"], b["i4"], b["mg"])
-    score_pass(b["wa"], b["wb"], b["g"], b["inv"], b["sc"])
-    softmax_pass(b["sc"], b["d"], b["c"])
-
-
 def load_forward(b):
     return lambda r, j: b["z"][pl.ds(r * 16 + j, SUB), :]
 
 
 def load_side(b):
     return lambda r, j: b["y"][j, pl.ds(r, SUB), :]
-def kernel(t_ref, g_ref, f_ref, s_ref, o_ref, *bufs):
-    b = dict(zip(SCRATCH, bufs))
+
+
+MESH = pl.DeviceIdType.MESH
+
+
+def kernel(chunks, t_ref, images_ref, out_ref, *refs):
+    names = list(SCRATCH)
+    b = dict(zip(names, refs))
+    own, f_in, s_in, stage, zeros, here, put, sent, got, copied = refs[len(names) :]
     perm = b["perm"]
+    axes = {"along": (lax.axis_index("along"), lax.axis_size("along")), "strip": (lax.axis_index("strip"), lax.axis_size("strip"))}
+
+    barrier = pltpu.get_barrier_semaphore()
+    for axis, (at, count) in axes.items():
+        for step in (1, count - 1):
+            pl.semaphore_signal(barrier, inc=1, device_id={axis: lax.rem(at + step, count)}, device_id_type=MESH)
+    load_own = pltpu.make_async_copy(images_ref, own, here)
+    load_own.start()
+    pl.semaphore_wait(barrier, 4)
+
+    def send(axis, step, src, dst, slot):
+        at, _ = axes[axis]
+        return pltpu.make_async_remote_copy(
+            src_ref=src, dst_ref=dst, send_sem=sent.at[slot], recv_sem=got.at[slot],
+            device_id={axis: at + step}, device_id_type=MESH)
+
+    plan = (("along", f_in, 0, 0), ("strip", s_in, 1, 4))
+    image_copies = []
+    for axis, landing, slot, _ in plan:
+        at, count = axes[axis]
+        copy = send(axis, -1, images_ref, landing, slot)
+        image_copies.append(copy)
+
+        @pl.when(at > 0)
+        def _():
+            copy.start()
+
+        @pl.when(at == count - 1)
+        def _():
+            landing[...] = jnp.zeros_like(landing)
+
+    zeros[...] = jnp.zeros_like(zeros)
     fill_perm(perm)
-    guide_fields(g_ref[...], perm[...], b["pad"], b["g"], b["a1"], b["a2"], b["i4"], b["mg"], b["inv"])
-    forward_table(f_ref[...], t_ref[0], perm[...], b["z"])
-    levels(load_forward(b), b)
-    o_ref[0] = gathered(b["d"], perm[...])
-    o_ref[1] = gathered(b["c"], perm[...])
-    side_table(s_ref[...], t_ref[1], perm[...], b["y"], b["pad"])
-    levels(load_side(b), b)
-    o_ref[2] = gathered(b["d"], perm[...])
-    o_ref[3] = gathered(b["c"], perm[...])
-
-def maps(t, g, f, s):
-    V = pl.BlockSpec(memory_space=pltpu.VMEM)
-    return pl.pallas_call(kernel, out_shape=jax.ShapeDtypeStruct((4, ROWS, COLS), F32),
-        in_specs=[pl.BlockSpec(memory_space=pltpu.SMEM), V, V, V], out_specs=V,
-        scratch_shapes=[pltpu.VMEM(*v) for v in SCRATCH.values()],
-        compiler_params=pltpu.CompilerParams(vmem_limit_bytes=60 << 20))(t, g, f, s)
-
-
-def from_behind(value, axis, steps):
-    count = lax.axis_size(axis)
-    leading, last = (max(0, -steps), min(count, count - steps))
-    return lax.ppermute(value, axis, [(source, source + steps) for source in range(leading, last)])
+    load_own.wait()
+    guide_fields(own[...], perm[...], b["pad"], b["g"], b["a1"], b["a2"], b["i4"], b["mg"], b["inv"])
+
+    slot = 2
+    waits, local = [], []
+    for which, (axis, landing, _, base) in enumerate(plan):
+        at, count = axes[axis]
+        image_copy = image_copies[which]
+        empty = pltpu.make_async_copy(zeros, out_ref.at[pl.ds(base + 2, 2)], copied.at[which])
+
+        @pl.when(at == 0)
+        def _():
+            empty.start()
+
+        @pl.when(at < count - 1)
+        def _():
+            image_copy.wait_recv()
+
+        if which == 0:
+            forward_table(landing[...], t_ref[0], perm[...], b["z"])
+            load = load_forward(b)
+        else:
+            side_table(landing[...], t_ref[1], perm[...], b["y"], b["pad"])
+            load = load_side(b)
+        cost_pass(load, b["g"], b["hx"], b["hy"])
+        coef_pass(b["hx"], b["hy"], b["wa"], b["wb"], b["a1"], b["a2"], b["i4"], b["mg"])
+        rows = ROWS // chunks[which]
+        for chunk in range(chunks[which]):
+            start = chunk * rows
+            score_pass(start, rows, b["wa"], b["wb"], b["g"], b["inv"], b["sc"])
+            softmax_pass(start, rows, b["sc"], b["d"], b["c"])
+            both = gathered(start, rows, (b["d"], b["c"]), perm[...])
+            span = pl.ds(start, rows)
+            stage[which, 0, span, :] = both[:rows]
+            stage[which, 1, span, :] = both[rows:]
+            source = stage.at[which, :, span, :]
+            mine = pltpu.make_async_copy(source, out_ref.at[pl.ds(base, 2), span, :], put.at[slot - 2])
+            mine.start()
+            local.append(mine)
+            copy = send(axis, 1, source, out_ref.at[pl.ds(base + 2, 2), span, :], slot)
+
+            @pl.when(at < count - 1)
+            def _():
+                copy.start()
+
+            waits.append((at, count, copy))
+            slot += 1
+
+    for which, (axis, _, _, base) in enumerate(plan):
+        at, count = axes[axis]
+        image_copy = image_copies[which]
+        empty = pltpu.make_async_copy(zeros, out_ref.at[pl.ds(base + 2, 2)], copied.at[which])
+
+        @pl.when(at > 0)
+        def _():
+            image_copy.wait_send()
+
+        @pl.when(at == 0)
+        def _():
+            empty.wait()
+
+    for mine in local:
+        mine.wait()
+    for at, count, copy in waits:
+
+        @pl.when(at < count - 1)
+        def _():
+            copy.wait_send()
+
+        @pl.when(at > 0)
+        def _():
+            copy.wait_recv()
+
+
+CHUNKS = (2, 4)
 
 
 def per_device(images, offsets):
-    forward = from_behind(images, "along", -1)
-    side = from_behind(images, "strip", -1)
-    own = maps(offsets.reshape(2), images, forward, side)
-    fwd_back = from_behind(own[0:2], "along", 1)
-    side_back = from_behind(own[2:4], "strip", 1)
-    return jnp.concatenate([own[0:2], fwd_back, own[2:4], side_back], axis=0)
+    pieces = sum(CHUNKS)
+    return pl.pallas_call(
+        functools.partial(kernel, CHUNKS),
+        out_shape=jax.ShapeDtypeStruct((8, ROWS, COLS), F32),
+        in_specs=[pl.BlockSpec(memory_space=pltpu.SMEM), pl.BlockSpec(memory_space=pl.ANY)],
+        out_specs=pl.BlockSpec(memory_space=pl.ANY),
+        scratch_shapes=[pltpu.VMEM(*v) for v in SCRATCH.values()]
+        + [pltpu.VMEM((ROWS, COLS), F32)] * 3
+        + [pltpu.VMEM((2, 2, ROWS, COLS), F32), pltpu.VMEM((2, ROWS, COLS), F32)]
+        + [
+            pltpu.SemaphoreType.DMA,
+            pltpu.SemaphoreType.DMA((pieces,)),
+            pltpu.SemaphoreType.DMA((2 + pieces,)),
+            pltpu.SemaphoreType.DMA((2 + pieces,)),
+            pltpu.SemaphoreType.DMA((2,)),
+        ],
+        compiler_params=pltpu.CompilerParams(collective_id=0, has_side_effects=True, vmem_limit_bytes=48 << 20),
+    )(offsets.reshape(2), images)
 
 
 def solution(mesh):

time: 45.1 us -> 29.3 us (0.65)
  the two profiles are of different devices: /device:TPU:108 before, /device:TPU:1 now
where the time goes in v1:
time: 29.3 us; the launch traced here: 29.2 us
  Pallas kernels  26.7 us (91%)
  local copies, waits for them, and re-layouts  2.53 us (9%)
    pallas_call x1, Pallas kernels, per_device(): pl.pallas_call(functools.partial(kernel, CHUNKS), out_shape=jax.ShapeDtyp...  26.7 us
    unnamed x5, local copies, waits for them, and re-layouts  2.53 us

profile of v1, /device:TPU:1, one launch (start us, length us, event | category | flops | bytes accessed | tf_op | source)
XLA Modules:
  0.0 29.2 jit_solution(7261494460312112807)
XLA Ops:
  0.0 0.0 copy-start.1
  0.0 0.7 %copy-done.1 = s32[1,1,2]{2,1,0:T(1,128)S(1)} copy-done((s32[1,1,2]{2,1,0:T(1,128)S(1)}, s32[1,1,2]{2,1,0:T(1,128)}, u32[]{:S(2)}) %copy-start.1) | copy-done | bytes 32
  0.7 0.0 copy-start
  0.7 0.9 %copy-done = f32[64,512]{1,0:T(8,128)S(1)} copy-done((f32[64,512]{1,0:T(8,128)S(1)}, f32[64,512]{1,0:T(8,128)}, u32[]{:S(2)}) %copy-start) | copy-done | bytes 131096
  1.6 26.7 %shard_map.28 = f32[8,64,512]{2,1,0:T(8,128)S(1)} custom-call(s32[2]{0:T(128)S(1)} %bitcast.1, f32[64,512]{1,0:T(8,128)S(1)} %copy-done), custom_call_target="tpu_custom_call" | custom-call | tf_op jit(solution)/shard_map/pallas_call | solution.py:395
  28.2 1.0 %copy.4 = f32[8,64,512]{2,1,0:T(8,128)} copy(f32[8,64,512]{2,1,0:T(8,128)S(1)} %shard_map.28) | data formatting | bytes 2097152
Async XLA Ops:
  0.0 0.7 %copy-start.1 = (s32[1,1,2]{2,1,0:T(1,128)S(1)}, s32[1,1,2]{2,1,0:T(1,128)}, u32[]{:S(2)}) copy-start(s32[1,1,2]{2,1,0:T(1,128)} %param.3) | copy-start | bytes 28
  0.7 0.9 %copy-start = (f32[64,512]{1,0:T(8,128)S(1)}, f32[64,512]{1,0:T(8,128)}, u32[]{:S(2)}) copy-start(f32[64,512]{1,0:T(8,128)} %images_ref.1) | copy-start | bytes 393220

commit v2 on v1

--- a/solution.py
+++ b/solution.py
@@ -12,6 +12,7 @@
 HALF = LANES // 2
 RADIUS = 4
 UNROLL = 16
+COST_UNROLL = 16
 SCALE = -4.0 * 1.4426950408889634
 
 
@@ -76,9 +77,10 @@
 
 def guide_fields(g, perm, pad_ref, g_ref, a1_ref, a2_ref, i4_ref, mg_ref, inv_ref):
     gd = spread(g, perm)
+    for j, v in enumerate(widened(gd)):
+        g_ref[j] = v
     zero = jnp.zeros((SUB, LANES), F32)
     for j in range(8):
-        g_ref[j] = gd[j]
         for n, field in enumerate((gd[j], gd[j] * gd[j])):
             at = 2 * j + n
             pad_ref[at, pl.ds(0, SUB), :] = zero
@@ -116,20 +118,37 @@
     lax.fori_loop(0, ROWS // SUB, tile, 0)
 
 
+def ends(shape):
+    pos = lane_ids(shape) & (HALF - 1)
+    return pos == 0, pos == HALF - 1
+
+
+def widened(x):
+    first, last = ends(x[0].shape)
+    before = [jnp.where(first, 0.0, pltpu.roll(v, 1, 1)) for v in x[4:]]
+    after = [jnp.where(last, 0.0, pltpu.roll(v, LANES - 1, 1)) for v in x[:4]]
+    return before + list(x) + after
+
+
+STEP = 24
+
+
 def forward_table(f, shift, perm, z_ref):
     base = spread(pltpu.roll(f, COLS - shift, 1), perm)
     low = lane_ids((ROWS, LANES)) < HALF
-    for e in range(8):
-        one = pltpu.roll(base[e], LANES - 1, 1)
-        two = pltpu.roll(one, LANES - 1, 1)
-        z_ref[pl.ds(e, ROWS, stride=16), :] = jnp.where(low, base[e], one)
-        z_ref[pl.ds(e + 8, ROWS, stride=16), :] = jnp.where(low, one, two)
-
-
-def side_table(s, shift, perm, y_ref, pad_ref):
-    base = spread(pltpu.roll(s, ROWS - shift, 0), perm)
+    turned = {(k, 0): base[k] for k in range(8)}
+    for k in range(8):
+        for q in ((-1,) if k >= 4 else ()) + (1, 2) + ((3,) if k < 3 else ()):
+            turned[k, q] = pltpu.roll(base[k], (-q) % LANES, 1)
+    for e in range(-4, 19):
+        q, k = divmod(e, 8)
+        z_ref[pl.ds(e + 4, ROWS, stride=STEP), :] = jnp.where(low, turned[k, q], turned[k, q + 1])
+
+
+def side_table(s, shift, perm, y_ref):
+    base = widened(spread(pltpu.roll(s, ROWS - shift, 0), perm))
     low = lane_ids((SUB, LANES)) < HALF
-    for j in range(8):
+    for j in range(16):
         tiles = [base[j][SUB * k : SUB * (k + 1)] for k in range(8)]
         for k in range(9):
             y_ref[j, pl.ds(SUB * k, SUB), :] = jnp.where(low, tiles[k % 8], tiles[(k + 1) % 8])
@@ -139,20 +158,36 @@
     return jnp.broadcast_to(ref[j, pl.ds(r, 1), :], (SUB, LANES))
 
 
-def cost_pass(load, g_ref, hx_ref, hy_ref):
+def wide_box(x):
+    suf = [x[7]]
+    for k in range(6, -1, -1):
+        suf.append(suf[-1] + x[k])
+    suf.reverse()
+    pre = [x[8]]
+    for k in range(9, 16):
+        pre.append(pre[-1] + x[k])
+    return [suf[j] + pre[j] for j in range(8)]
+
+
+def cost_pass(load, masked, g_ref, hx_ref, hy_ref):
     def row(r, carry):
+        first, last = ends((SUB, LANES))
         xs, ys = [], []
-        for j in range(8):
+        for j in range(16):
             g = bcast(g_ref, j, r)
             x = jnp.abs(g - load(r, j))
+            if masked and j < 4:
+                x = jnp.where(first, 0.0, x)
+            if masked and j >= 12:
+                x = jnp.where(last, 0.0, x)
             xs.append(x)
             ys.append(g * x)
         for ref, vals in ((hx_ref, xs), (hy_ref, ys)):
-            for j, v in enumerate(row_box(vals)):
+            for j, v in enumerate(wide_box(vals)):
                 ref[j, r] = v
         return carry
 
-    lax.fori_loop(0, ROWS, row, 0, unroll=UNROLL)
+    lax.fori_loop(0, ROWS, row, 0, unroll=COST_UNROLL)
 
 
 def coef_pass(hx_ref, hy_ref, wa_ref, wb_ref, a1_ref, a2_ref, i4_ref, mg_ref):
@@ -206,10 +241,10 @@
         ha = row_box([wa_ref[j, r] for j in range(8)])
         hb = row_box([wb_ref[j, r] for j in range(8)])
         for j in range(8):
-            sc_ref[r, pl.ds(SUB * j, SUB), :] = (ha[j] * bcast(g_ref, j, r) + hb[j]) * bcast(inv_ref, j, r)
+            sc_ref[r, pl.ds(SUB * j, SUB), :] = (ha[j] * bcast(g_ref, j + 4, r) + hb[j]) * bcast(inv_ref, j, r)
         return carry
 
-    lax.fori_loop(0, rows, row, 0, unroll=min(UNROLL, rows))
+    lax.fori_loop(0, rows, row, 0, unroll=min(32, rows))
 
 
 def softmax_pass(start, rows, sc_ref, d_ref, c_ref):
@@ -255,9 +290,9 @@
 
 SCRATCH = dict(
     perm=((COLS, COLS), BF16), pad=((16, ROWS + 16, LANES), F32),
-    g=((8, ROWS, LANES), F32), a1=((8, ROWS, LANES), F32), a2=((8, ROWS, LANES), F32),
-    i4=((8, ROWS, LANES), F32), mg=((8, ROWS, LANES), F32), inv=((8, ROWS, LANES), F32),
-    z=((16 * ROWS, LANES), F32), y=((8, ROWS + SUB, LANES), F32),
+    g=((16, ROWS, LANES), F32), a1=((8, ROWS, LANES), F32), a2=((8, ROWS, LANES), F32),
+    i4=((8, ROWS, LANES), F32), mg=((16, ROWS, LANES), F32), inv=((8, ROWS, LANES), F32),
+    z=((24 * ROWS, LANES), F32), y=((16, ROWS + SUB, LANES), F32),
     hx=((8, ROWS, SUB, LANES), F32), hy=((8, ROWS, SUB, LANES), F32),
     wa=((8, ROWS, SUB, LANES), F32), wb=((8, ROWS, SUB, LANES), F32),
     sc=((ROWS, SUB * SUB, LANES), F32), d=((ROWS * SUB, LANES), F32), c=((ROWS * SUB, LANES), F32),
@@ -265,7 +300,7 @@
 
 
 def load_forward(b):
-    return lambda r, j: b["z"][pl.ds(r * 16 + j, SUB), :]
+    return lambda r, j: b["z"][pl.ds(r * STEP + j, SUB), :]
 
 
 def load_side(b):
@@ -273,22 +308,45 @@
 
 
 MESH = pl.DeviceIdType.MESH
-
-
-def kernel(chunks, t_ref, images_ref, out_ref, *refs):
+CHUNKS = (2, 4)
+
+
+def kernel(offsets_ref, images_ref, out_ref, *refs):
     names = list(SCRATCH)
     b = dict(zip(names, refs))
-    own, f_in, s_in, stage, zeros, here, put, sent, got, copied = refs[len(names) :]
+    own, f_in, s_in, shifts, here, sent, got = refs[len(names) :]
     perm = b["perm"]
-    axes = {"along": (lax.axis_index("along"), lax.axis_size("along")), "strip": (lax.axis_index("strip"), lax.axis_size("strip"))}
+    axes = {name: (lax.axis_index(name), lax.axis_size(name)) for name in ("along", "strip")}
 
     barrier = pltpu.get_barrier_semaphore()
+    ready = 0
     for axis, (at, count) in axes.items():
-        for step in (1, count - 1):
-            pl.semaphore_signal(barrier, inc=1, device_id={axis: lax.rem(at + step, count)}, device_id_type=MESH)
-    load_own = pltpu.make_async_copy(images_ref, own, here)
+        for step in (1, -1):
+            inside = jnp.logical_and(at + step >= 0, at + step < count)
+            ready = ready + inside.astype(jnp.int32)
+
+            @pl.when(inside)
+            def _():
+                pl.semaphore_signal(barrier, inc=1, device_id={axis: at + step}, device_id_type=MESH)
+
+    load_own = pltpu.make_async_copy(images_ref, own, here.at[0])
     load_own.start()
-    pl.semaphore_wait(barrier, 4)
+    load_shifts = pltpu.make_async_copy(offsets_ref, shifts, here.at[1])
+    load_shifts.start()
+    fill_perm(perm)
+    plan = (("along", f_in, 0), ("strip", s_in, 4))
+    for axis, landing, base in plan:
+        at, count = axes[axis]
+
+        @pl.when(at == count - 1)
+        def _():
+            landing[...] = jnp.zeros_like(landing)
+
+        @pl.when(at == 0)
+        def _():
+            out_ref[pl.ds(base + 2, 2)] = jnp.zeros((2, ROWS, COLS), F32)
+
+    pl.semaphore_wait(barrier, ready)
 
     def send(axis, step, src, dst, slot):
         at, _ = axes[axis]
@@ -296,119 +354,76 @@
             src_ref=src, dst_ref=dst, send_sem=sent.at[slot], recv_sem=got.at[slot],
             device_id={axis: at + step}, device_id_type=MESH)
 
-    plan = (("along", f_in, 0, 0), ("strip", s_in, 1, 4))
-    image_copies = []
-    for axis, landing, slot, _ in plan:
+    image_copies = [send(axis, -1, images_ref, landing, slot) for slot, (axis, landing, _) in enumerate(plan)]
+
+    def start_image(which, also=True):
+        at, _ = axes[plan[which][0]]
+        pl.when(jnp.logical_and(at > 0, also))(image_copies[which].start)
+
+    def await_image(which):
+        at, count = axes[plan[which][0]]
+        pl.when(at < count - 1)(image_copies[which].wait_recv)
+
+    near = lax.rem(axes["along"][0], 2) == 1
+    start_image(0)
+    start_image(1, near)
+    load_own.wait()
+    load_shifts.wait()
+    guide_fields(own[...], perm[...], b["pad"], b["g"], b["a1"], b["a2"], b["i4"], b["mg"], b["inv"])
+    pl.when(axes["along"][0] > 0)(image_copies[0].wait_send)
+    start_image(1, jnp.logical_not(near))
+    await_image(0)
+
+    slot = 2
+    waits = []
+    for which, (axis, landing, base) in enumerate(plan):
         at, count = axes[axis]
-        copy = send(axis, -1, images_ref, landing, slot)
-        image_copies.append(copy)
-
-        @pl.when(at > 0)
-        def _():
-            copy.start()
-
-        @pl.when(at == count - 1)
-        def _():
-            landing[...] = jnp.zeros_like(landing)
-
-    zeros[...] = jnp.zeros_like(zeros)
-    fill_perm(perm)
-    load_own.wait()
-    guide_fields(own[...], perm[...], b["pad"], b["g"], b["a1"], b["a2"], b["i4"], b["mg"], b["inv"])
-
-    slot = 2
-    waits, local = [], []
-    for which, (axis, landing, _, base) in enumerate(plan):
-        at, count = axes[axis]
-        image_copy = image_copies[which]
-        empty = pltpu.make_async_copy(zeros, out_ref.at[pl.ds(base + 2, 2)], copied.at[which])
-
-        @pl.when(at == 0)
-        def _():
-            empty.start()
-
-        @pl.when(at < count - 1)
-        def _():
-            image_copy.wait_recv()
-
         if which == 0:
-            forward_table(landing[...], t_ref[0], perm[...], b["z"])
+            forward_table(landing[...], shifts[0, 0, 0], perm[...], b["z"])
             load = load_forward(b)
         else:
-            side_table(landing[...], t_ref[1], perm[...], b["y"], b["pad"])
+            await_image(1)
+            side_table(landing[...], shifts[0, 0, 1], perm[...], b["y"])
             load = load_side(b)
-        cost_pass(load, b["g"], b["hx"], b["hy"])
+        cost_pass(load, which == 0, b["g"], b["hx"], b["hy"])
         coef_pass(b["hx"], b["hy"], b["wa"], b["wb"], b["a1"], b["a2"], b["i4"], b["mg"])
-        rows = ROWS // chunks[which]
-        for chunk in range(chunks[which]):
+        rows = ROWS // CHUNKS[which]
+        for chunk in range(CHUNKS[which]):
             start = chunk * rows
             score_pass(start, rows, b["wa"], b["wb"], b["g"], b["inv"], b["sc"])
             softmax_pass(start, rows, b["sc"], b["d"], b["c"])
             both = gathered(start, rows, (b["d"], b["c"]), perm[...])
             span = pl.ds(start, rows)
-            stage[which, 0, span, :] = both[:rows]
-            stage[which, 1, span, :] = both[rows:]
-            source = stage.at[which, :, span, :]
-            mine = pltpu.make_async_copy(source, out_ref.at[pl.ds(base, 2), span, :], put.at[slot - 2])
-            mine.start()
-            local.append(mine)
-            copy = send(axis, 1, source, out_ref.at[pl.ds(base + 2, 2), span, :], slot)
-
-            @pl.when(at < count - 1)
-            def _():
-                copy.start()
-
+            out_ref[base, span, :] = both[:rows]
+            out_ref[base + 1, span, :] = both[rows:]
+            copy = send(axis, 1, out_ref.at[pl.ds(base, 2), span, :], out_ref.at[pl.ds(base + 2, 2), span, :], slot)
+            pl.when(at < count - 1)(copy.start)
             waits.append((at, count, copy))
             slot += 1
 
-    for which, (axis, _, _, base) in enumerate(plan):
-        at, count = axes[axis]
-        image_copy = image_copies[which]
-        empty = pltpu.make_async_copy(zeros, out_ref.at[pl.ds(base + 2, 2)], copied.at[which])
-
-        @pl.when(at > 0)
-        def _():
-            image_copy.wait_send()
-
-        @pl.when(at == 0)
-        def _():
-            empty.wait()
-
-    for mine in local:
-        mine.wait()
+    pl.when(axes["strip"][0] > 0)(image_copies[1].wait_send)
     for at, count, copy in waits:
-
-        @pl.when(at < count - 1)
-        def _():
-            copy.wait_send()
-
-        @pl.when(at > 0)
-        def _():
-            copy.wait_recv()
-
-
-CHUNKS = (2, 4)
+        pl.when(at < count - 1)(copy.wait_send)
+        pl.when(at > 0)(copy.wait_recv)
 
 
 def per_device(images, offsets):
-    pieces = sum(CHUNKS)
+    slots = 2 + sum(CHUNKS)
     return pl.pallas_call(
-        functools.partial(kernel, CHUNKS),
+        kernel,
         out_shape=jax.ShapeDtypeStruct((8, ROWS, COLS), F32),
-        in_specs=[pl.BlockSpec(memory_space=pltpu.SMEM), pl.BlockSpec(memory_space=pl.ANY)],
-        out_specs=pl.BlockSpec(memory_space=pl.ANY),
+        in_specs=[pl.BlockSpec(memory_space=pltpu.HBM), pl.BlockSpec(memory_space=pltpu.HBM)],
+        out_specs=pl.BlockSpec(memory_space=pltpu.VMEM),
         scratch_shapes=[pltpu.VMEM(*v) for v in SCRATCH.values()]
         + [pltpu.VMEM((ROWS, COLS), F32)] * 3
-        + [pltpu.VMEM((2, 2, ROWS, COLS), F32), pltpu.VMEM((2, ROWS, COLS), F32)]
         + [
-            pltpu.SemaphoreType.DMA,
-            pltpu.SemaphoreType.DMA((pieces,)),
-            pltpu.SemaphoreType.DMA((2 + pieces,)),
-            pltpu.SemaphoreType.DMA((2 + pieces,)),
+            pltpu.SMEM((1, 1, 2), jnp.int32),
             pltpu.SemaphoreType.DMA((2,)),
+            pltpu.SemaphoreType.DMA((slots,)),
+            pltpu.SemaphoreType.DMA((slots,)),
         ],
         compiler_params=pltpu.CompilerParams(collective_id=0, has_side_effects=True, vmem_limit_bytes=48 << 20),
-    )(offsets.reshape(2), images)
+    )(pltpu.with_memory_space_constraint(offsets, pltpu.HBM), pltpu.with_memory_space_constraint(images, pltpu.HBM))
 
 
 def solution(mesh):

time: 29.3 us -> 24.8 us (0.85)
  the two profiles are of different devices: /device:TPU:1 before, /device:TPU:103 now
where the time goes in v2:
time: 24.8 us; the launch traced here: 24.7 us
  Pallas kernels  23.7 us (96%)
  local copies, waits for them, and re-layouts  0.97 us (4%)
    pallas_call x1, Pallas kernels, per_device(): pl.pallas_call(kernel, out_shape=jax.ShapeDtypeStruct((8, ROWS, COLS), F3...  23.7 us
    unnamed x1, local copies, waits for them, and re-layouts  0.97 us

profile of v2, /device:TPU:103, one launch (start us, length us, event | category | flops | bytes accessed | tf_op | source)
XLA Modules:
  0.0 24.7 jit_solution(17049499787681395352)
XLA Ops:
  0.0 23.7 %shard_map.28 = f32[8,64,512]{2,1,0:T(8,128)S(1)} custom-call(s32[1,1,2]{2,1,0:T(1,128)} %offsets_ref.1, f32[64,512]{1,0:T(8,128)} %images_ref.1), custom_call_target="tpu_custom_call" | custom-call | tf_op jit(solution)/shard_map/pallas_call | solution.py:412
  23.7 1.0 %copy.4 = f32[8,64,512]{2,1,0:T(8,128)} copy(f32[8,64,512]{2,1,0:T(8,128)S(1)} %shard_map.28) | data formatting | bytes 2097152

commit v3 on v2

--- a/solution.py
+++ b/solution.py
@@ -28,24 +28,24 @@
     return jnp.concatenate([hi, mid, low], axis=0)
 
 
-def permuted(x, perm, transposed):
+def permuted(x, perm):
     n = x.shape[0]
-    dims = (((1,), (1 if transposed else 0,)), ((), ()))
-    out = lax.dot_general(split3(x), perm, dims, preferred_element_type=F32)
+    out = jnp.dot(split3(x), perm, preferred_element_type=F32)
     return out[:n] + out[n : 2 * n] + out[2 * n :]
 
 
-def fill_perm(perm_ref):
+def fill_perm(perm_ref, back_ref):
     for k in range(4):
         shape = (128, COLS)
-        n = lax.broadcasted_iota(jnp.int32, shape, 1)
-        c = lax.broadcasted_iota(jnp.int32, shape, 0) + 128 * k
-        hit = c == 8 * (n & 63) + (n >> 6)
-        perm_ref[pl.ds(128 * k, 128), :] = jnp.where(hit, 1.0, 0.0).astype(BF16)
+        along = lax.broadcasted_iota(jnp.int32, shape, 1)
+        down = lax.broadcasted_iota(jnp.int32, shape, 0) + 128 * k
+        rows = pl.ds(128 * k, 128)
+        perm_ref[rows, :] = jnp.where(down == 8 * (along & 63) + (along >> 6), 1.0, 0.0).astype(BF16)
+        back_ref[rows, :] = jnp.where(along == 8 * (down & 63) + (down >> 6), 1.0, 0.0).astype(BF16)
 
 
 def spread(x, perm):
-    y = permuted(x, perm, False)
+    y = permuted(x, perm)
     low = lane_ids((x.shape[0], LANES)) < HALF
     out = []
     for k in range(4):
@@ -75,7 +75,7 @@
     return out
 
 
-def guide_fields(g, perm, pad_ref, g_ref, a1_ref, a2_ref, i4_ref, mg_ref, inv_ref):
+def guide_fields(g, perm, pad_ref, g_ref, a1_ref, a2_ref, i4_ref, mg_ref, inv_ref, then):
     gd = spread(g, perm)
     for j, v in enumerate(widened(gd)):
         g_ref[j] = v
@@ -86,6 +86,8 @@
             pad_ref[at, pl.ds(0, SUB), :] = zero
             pad_ref[at, pl.ds(SUB, ROWS), :] = field
             pad_ref[at, pl.ds(SUB + ROWS, SUB), :] = zero
+
+    then()
 
     def tile(i, carry):
         base = pl.multiple_of(i * SUB, SUB)
@@ -235,27 +237,46 @@
     lax.fori_loop(0, 8, column, 0)
 
 
+def running(x):
+    head = [x[0]]
+    for k in range(1, 8):
+        head.append(head[-1] + x[k])
+    tail = [head[7]] + [None] * 6 + [x[7]]
+    for k in range(6, 0, -1):
+        tail[k] = tail[k + 1] + x[k]
+    return head, tail
+
+
 def score_pass(start, rows, wa_ref, wb_ref, g_ref, inv_ref, sc_ref):
     def row(i, carry):
         r = start + i
-        ha = row_box([wa_ref[j, r] for j in range(8)])
-        hb = row_box([wb_ref[j, r] for j in range(8)])
+        first, last = ends((SUB, LANES))
+        ha, ta = running([wa_ref[j, r] for j in range(8)])
+        hb, tb = running([wb_ref[j, r] for j in range(8)])
         for j in range(8):
-            sc_ref[r, pl.ds(SUB * j, SUB), :] = (ha[j] * bcast(g_ref, j + 4, r) + hb[j]) * bcast(inv_ref, j, r)
-        return carry
-
-    lax.fori_loop(0, rows, row, 0, unroll=min(32, rows))
+            if j < 4:
+                other = ta[j + 4] * bcast(g_ref, j + 12, r) + tb[j + 4]
+                other = jnp.where(first, 0.0, pltpu.roll(other, 1, 1))
+                same = ha[j + 4] * bcast(g_ref, j + 4, r) + hb[j + 4]
+            else:
+                other = ha[j - 4] * bcast(g_ref, j - 4, r) + hb[j - 4]
+                other = jnp.where(last, 0.0, pltpu.roll(other, LANES - 1, 1))
+                same = ta[j - 4] * bcast(g_ref, j + 4, r) + tb[j - 4]
+            sc_ref[r, pl.ds(j, SUB, stride=SUB), :] = (same + other) * bcast(inv_ref, j, r)
+        return carry
+
+    lax.fori_loop(0, rows, row, 0, unroll=min(UNROLL, rows))
 
 
 def softmax_pass(start, rows, sc_ref, d_ref, c_ref):
     def row(i, carry):
         r = start + i
         high = lane_ids((SUB, LANES)) >= HALF
-        t = [sc_ref[r, pl.ds(s, SUB, stride=SUB), :] for s in range(8)]
-        top = t[0]
-        for s in range(1, 8):
-            top = jnp.maximum(top, t[s])
-        top = jnp.maximum(top, pltpu.roll(top, HALF, 1))
+        t = [sc_ref[r, pl.ds(SUB * s, SUB), :] for s in range(8)]
+        top = t
+        while len(top) > 1:
+            top = [jnp.maximum(top[k], top[k + 1]) for k in range(0, len(top), 2)]
+        top = jnp.maximum(top[0], pltpu.roll(top[0], HALF, 1))
         total = lift = square = None
         for s in range(7, -1, -1):
             w = jnp.exp2(t[s] - top)
@@ -285,11 +306,11 @@
             odd = ref[pl.ds(SUB * start + 2 * k + 1, rows, stride=SUB), :]
             parts.append(jnp.where(low, even, odd))
         stacked.append(jnp.concatenate(parts, axis=1))
-    return permuted(jnp.concatenate(stacked, axis=0), perm, True)
+    return permuted(jnp.concatenate(stacked, axis=0), perm)
 
 
 SCRATCH = dict(
-    perm=((COLS, COLS), BF16), pad=((16, ROWS + 16, LANES), F32),
+    perm=((COLS, COLS), BF16), back=((COLS, COLS), BF16), pad=((16, ROWS + 16, LANES), F32),
     g=((16, ROWS, LANES), F32), a1=((8, ROWS, LANES), F32), a2=((8, ROWS, LANES), F32),
     i4=((8, ROWS, LANES), F32), mg=((16, ROWS, LANES), F32), inv=((8, ROWS, LANES), F32),
     z=((24 * ROWS, LANES), F32), y=((16, ROWS + SUB, LANES), F32),
@@ -308,7 +329,7 @@
 
 
 MESH = pl.DeviceIdType.MESH
-CHUNKS = (2, 4)
+PIECES = 4
 
 
 def kernel(offsets_ref, images_ref, out_ref, *refs):
@@ -319,21 +340,17 @@
     axes = {name: (lax.axis_index(name), lax.axis_size(name)) for name in ("along", "strip")}
 
     barrier = pltpu.get_barrier_semaphore()
-    ready = 0
     for axis, (at, count) in axes.items():
-        for step in (1, -1):
-            inside = jnp.logical_and(at + step >= 0, at + step < count)
-            ready = ready + inside.astype(jnp.int32)
-
-            @pl.when(inside)
-            def _():
-                pl.semaphore_signal(barrier, inc=1, device_id={axis: at + step}, device_id_type=MESH)
+
+        @pl.when(at < count - 1)
+        def _():
+            pl.semaphore_signal(barrier, inc=1, device_id={axis: at + 1}, device_id_type=MESH)
 
     load_own = pltpu.make_async_copy(images_ref, own, here.at[0])
     load_own.start()
     load_shifts = pltpu.make_async_copy(offsets_ref, shifts, here.at[1])
     load_shifts.start()
-    fill_perm(perm)
+    fill_perm(perm, b["back"])
     plan = (("along", f_in, 0), ("strip", s_in, 4))
     for axis, landing, base in plan:
         at, count = axes[axis]
@@ -346,7 +363,12 @@
         def _():
             out_ref[pl.ds(base + 2, 2)] = jnp.zeros((2, ROWS, COLS), F32)
 
-    pl.semaphore_wait(barrier, ready)
+    ready = sum((at > 0).astype(jnp.int32) for at, _ in axes.values())
+
+    @pl.when(ready > 0)
+    def _():
+        pl.semaphore_wait(barrier, ready)
+
 
     def send(axis, step, src, dst, slot):
         at, _ = axes[axis]
@@ -364,51 +386,68 @@
         at, count = axes[plan[which][0]]
         pl.when(at < count - 1)(image_copies[which].wait_recv)
 
-    near = lax.rem(axes["along"][0], 2) == 1
-    start_image(0)
-    start_image(1, near)
+    odd = lax.rem(axes["along"][0], 2)
+    start_image(0, odd == 1)
+    start_image(1, odd == 1)
     load_own.wait()
     load_shifts.wait()
-    guide_fields(own[...], perm[...], b["pad"], b["g"], b["a1"], b["a2"], b["i4"], b["mg"], b["inv"])
-    pl.when(axes["along"][0] > 0)(image_copies[0].wait_send)
-    start_image(1, jnp.logical_not(near))
-    await_image(0)
-
-    slot = 2
-    waits = []
-    for which, (axis, landing, base) in enumerate(plan):
-        at, count = axes[axis]
-        if which == 0:
-            forward_table(landing[...], shifts[0, 0, 0], perm[...], b["z"])
-            load = load_forward(b)
-        else:
+    guide_fields(own[...], perm[...], b["pad"], b["g"], b["a1"], b["a2"], b["i4"], b["mg"], b["inv"], lambda: start_image(0, odd == 0))
+    rows = ROWS // PIECES
+
+    def piece_copy(which, piece):
+        axis, _, base = plan[which]
+        span = pl.ds(pl.multiple_of(piece * rows, rows), rows)
+        return send(
+            axis, 1, out_ref.at[pl.ds(base, 2), span, :], out_ref.at[pl.ds(base + 2, 2), span, :],
+            2 + which * PIECES + piece)
+
+    def pair(step, carry):
+        which = lax.rem(step + odd, 2)
+
+        @pl.when(which == 0)
+        def _():
+            await_image(0)
+            forward_table(f_in[...], shifts[0, 0, 0], perm[...], b["z"])
+            start_image(1, odd == 0)
+            cost_pass(load_forward(b), True, b["g"], b["hx"], b["hy"])
+
+        @pl.when(which == 1)
+        def _():
             await_image(1)
-            side_table(landing[...], shifts[0, 0, 1], perm[...], b["y"])
-            load = load_side(b)
-        cost_pass(load, which == 0, b["g"], b["hx"], b["hy"])
+            side_table(s_in[...], shifts[0, 0, 1], perm[...], b["y"])
+            cost_pass(load_side(b), False, b["g"], b["hx"], b["hy"])
+
         coef_pass(b["hx"], b["hy"], b["wa"], b["wb"], b["a1"], b["a2"], b["i4"], b["mg"])
-        rows = ROWS // CHUNKS[which]
-        for chunk in range(CHUNKS[which]):
-            start = chunk * rows
+
+        def piece_of(piece, inner):
+            start = pl.multiple_of(piece * rows, rows)
             score_pass(start, rows, b["wa"], b["wb"], b["g"], b["inv"], b["sc"])
             softmax_pass(start, rows, b["sc"], b["d"], b["c"])
-            both = gathered(start, rows, (b["d"], b["c"]), perm[...])
+            both = gathered(start, rows, (b["d"], b["c"]), b["back"][...])
             span = pl.ds(start, rows)
-            out_ref[base, span, :] = both[:rows]
-            out_ref[base + 1, span, :] = both[rows:]
-            copy = send(axis, 1, out_ref.at[pl.ds(base, 2), span, :], out_ref.at[pl.ds(base + 2, 2), span, :], slot)
-            pl.when(at < count - 1)(copy.start)
-            waits.append((at, count, copy))
-            slot += 1
-
-    pl.when(axes["strip"][0] > 0)(image_copies[1].wait_send)
-    for at, count, copy in waits:
-        pl.when(at < count - 1)(copy.wait_send)
-        pl.when(at > 0)(copy.wait_recv)
+            out_ref[4 * which, span, :] = both[:rows]
+            out_ref[4 * which + 1, span, :] = both[rows:]
+            for k, (axis, _, _) in enumerate(plan):
+                at, count = axes[axis]
+                pl.when(jnp.logical_and(which == k, at < count - 1))(piece_copy(k, piece).start)
+            return inner
+
+        lax.fori_loop(0, PIECES, piece_of, 0)
+        return carry
+
+    lax.fori_loop(0, 2, pair, 0)
+
+    for which, (axis, _, _) in enumerate(plan):
+        at, count = axes[axis]
+        pl.when(at > 0)(image_copies[which].wait_send)
+        for piece in range(PIECES):
+            copy = piece_copy(which, piece)
+            pl.when(at < count - 1)(copy.wait_send)
+            pl.when(at > 0)(copy.wait_recv)
 
 
 def per_device(images, offsets):
-    slots = 2 + sum(CHUNKS)
+    slots = 2 + 2 * PIECES
     return pl.pallas_call(
         kernel,
         out_shape=jax.ShapeDtypeStruct((8, ROWS, COLS), F32),

time: 24.8 us -> 23.1 us (0.931)
  the two profiles are of different devices: /device:TPU:103 before, /device:TPU:102 now
where the time goes in v3:
time: 23.1 us; the launch traced here: 23 us
  Pallas kernels  22 us (95%)
  local copies, waits for them, and re-layouts  0.97 us (4%)
    pallas_call x1, Pallas kernels, per_device(): pl.pallas_call(kernel, out_shape=jax.ShapeDtypeStruct((8, ROWS, COLS), F3...  22 us
    unnamed x1, local copies, waits for them, and re-layouts  0.97 us

profile of v3, /device:TPU:102, one launch (start us, length us, event | category | flops | bytes accessed | tf_op | source)
XLA Modules:
  0.0 23.0 jit_solution(17314396131787822504)
XLA Ops:
  0.0 22.0 %shard_map.28 = f32[8,64,512]{2,1,0:T(8,128)S(1)} custom-call(s32[1,1,2]{2,1,0:T(1,128)} %offsets_ref.1, f32[64,512]{1,0:T(8,128)} %images_ref.1), custom_call_target="tpu_custom_call" | custom-call | tf_op jit(solution)/shard_map/pallas_call | solution.py:451
  22.0 1.0 %copy.4 = f32[8,64,512]{2,1,0:T(8,128)} copy(f32[8,64,512]{2,1,0:T(8,128)S(1)} %shard_map.28) | data formatting | bytes 2097152

commit v4 on v3

--- a/solution.py
+++ b/solution.py
@@ -12,7 +12,8 @@
 HALF = LANES // 2
 RADIUS = 4
 UNROLL = 16
-COST_UNROLL = 16
+COST_ROWS = 16
+FIRST_BLOCK = 1
 SCALE = -4.0 * 1.4426950408889634
 
 
@@ -171,8 +172,8 @@
     return [suf[j] + pre[j] for j in range(8)]
 
 
-def cost_pass(load, masked, g_ref, hx_ref, hy_ref):
-    def row(r, carry):
+def cost_pass(block, load, masked, g_ref, hx_ref, hy_ref):
+    def row(r):
         first, last = ends((SUB, LANES))
         xs, ys = [], []
         for j in range(16):
@@ -187,49 +188,50 @@
         for ref, vals in ((hx_ref, xs), (hy_ref, ys)):
             for j, v in enumerate(wide_box(vals)):
                 ref[j, r] = v
+
+    def rows_of(k, carry):
+        for i in range(COST_ROWS):
+            row(k * COST_ROWS + i)
         return carry
 
-    lax.fori_loop(0, ROWS, row, 0, unroll=COST_UNROLL)
-
-
-def coef_pass(hx_ref, hy_ref, wa_ref, wb_ref, a1_ref, a2_ref, i4_ref, mg_ref):
+    lax.fori_loop(block, ROWS // COST_ROWS, rows_of, 0)
+
+
+def coef_pass(top, hx_ref, hy_ref, wa_ref, wb_ref, a1_ref, a2_ref, i4_ref, mg_ref):
+    low = max(top - RADIUS, 0)
+    base = max(low - RADIUS, 0)
+
     def column(j, carry):
-        def window(ref):
-            total = ref[j, 0]
-            for r in range(1, RADIUS):
-                total = total + ref[j, r]
-            return total
-
-        p, q = window(hx_ref), window(hy_ref)
-        olda, oldb = [], []
+        p, q = hx_ref[j, base], hy_ref[j, base]
+        for r in range(base + 1, low + RADIUS):
+            p, q = p + hx_ref[j, r], q + hy_ref[j, r]
+        old = {}
         wa = wb = None
-        for r in range(ROWS + RADIUS):
+        for r in range(low, ROWS + RADIUS):
+            gone = r - 2 * RADIUS - 1
             if r < ROWS:
-                if r + RADIUS < ROWS:
-                    if r > RADIUS:
-                        p = p + (hx_ref[j, r + RADIUS] - hx_ref[j, r - RADIUS - 1])
-                        q = q + (hy_ref[j, r + RADIUS] - hy_ref[j, r - RADIUS - 1])
-                    else:
-                        p = p + hx_ref[j, r + RADIUS]
-                        q = q + hy_ref[j, r + RADIUS]
+                enter, leave = r + RADIUS < ROWS, r - RADIUS - 1 >= base
+                if enter and leave:
+                    p = p + (hx_ref[j, r + RADIUS] - hx_ref[j, r - RADIUS - 1])
+                    q = q + (hy_ref[j, r + RADIUS] - hy_ref[j, r - RADIUS - 1])
+                elif enter:
+                    p = p + hx_ref[j, r + RADIUS]
+                    q = q + hy_ref[j, r + RADIUS]
                 else:
                     p = p - hx_ref[j, r - RADIUS - 1]
                     q = q - hy_ref[j, r - RADIUS - 1]
                 ca = q * bcast(a1_ref, j, r) - p * bcast(a2_ref, j, r)
                 cb = p * bcast(i4_ref, j, r) - ca * bcast(mg_ref, j, r)
-                olda.append(ca)
-                oldb.append(cb)
-                if r == 0:
+                old[r] = ca, cb
+                if r == low:
                     wa, wb = ca, cb
-                elif r > 2 * RADIUS:
-                    wa = wa + (ca - olda[r - 2 * RADIUS - 1])
-                    wb = wb + (cb - oldb[r - 2 * RADIUS - 1])
+                elif gone >= low:
+                    wa, wb = wa + (ca - old[gone][0]), wb + (cb - old[gone][1])
                 else:
                     wa, wb = wa + ca, wb + cb
             else:
-                wa = wa - olda[r - 2 * RADIUS - 1]
-                wb = wb - oldb[r - 2 * RADIUS - 1]
-            if r >= RADIUS:
+                wa, wb = wa - old[gone][0], wb - old[gone][1]
+            if r - RADIUS >= top:
                 wa_ref[j, r - RADIUS] = wa
                 wb_ref[j, r - RADIUS] = wb
         return carry
@@ -330,12 +332,13 @@
 
 MESH = pl.DeviceIdType.MESH
 PIECES = 4
+SENT = 2
 
 
 def kernel(offsets_ref, images_ref, out_ref, *refs):
     names = list(SCRATCH)
     b = dict(zip(names, refs))
-    own, f_in, s_in, shifts, here, sent, got = refs[len(names) :]
+    own, f_in, s_in, b_in, b_shift, shifts, back_shifts, here, sent, got = refs[len(names) :]
     perm = b["perm"]
     axes = {name: (lax.axis_index(name), lax.axis_size(name)) for name in ("along", "strip")}
 
@@ -393,6 +396,13 @@
     load_shifts.wait()
     guide_fields(own[...], perm[...], b["pad"], b["g"], b["a1"], b["a2"], b["i4"], b["mg"], b["inv"], lambda: start_image(0, odd == 0))
     rows = ROWS // PIECES
+    along, alongs = axes["along"]
+    gives_back = jnp.logical_and(odd == 1, along < alongs - 1)
+    gets_back = jnp.logical_and(odd == 0, along > 0)
+    back_copies = [
+        send("along", 1, images_ref, b_in, 2 + 2 * PIECES),
+        send("along", 1, offsets_ref, b_shift, 3 + 2 * PIECES),
+    ]
 
     def piece_copy(which, piece):
         axis, _, base = plan[which]
@@ -401,23 +411,54 @@
             axis, 1, out_ref.at[pl.ds(base, 2), span, :], out_ref.at[pl.ds(base + 2, 2), span, :],
             2 + which * PIECES + piece)
 
-    def pair(step, carry):
-        which = lax.rem(step + odd, 2)
-
-        @pl.when(which == 0)
+    def pair(step):
+        which = jnp.where(step == 2, 2, lax.rem(step + odd, 2))
+
+        @pl.when(jnp.logical_and(step == 0, odd == 0))
         def _():
             await_image(0)
-            forward_table(f_in[...], shifts[0, 0, 0], perm[...], b["z"])
-            start_image(1, odd == 0)
-            cost_pass(load_forward(b), True, b["g"], b["hx"], b["hy"])
+
+        @pl.when(which == 2)
+        def _():
+            for copy in back_copies:
+                copy.wait_recv()
+            local = pltpu.make_async_copy(b_shift, back_shifts, here.at[2])
+            local.start()
+            f_in[...] = own[...]
+            local.wait()
+            guide_fields(b_in[...], perm[...], b["pad"], b["g"], b["a1"], b["a2"], b["i4"], b["mg"], b["inv"], lambda: None)
+
+        @pl.when(which != 1)
+        def _():
+            shift = jnp.where(which == 2, back_shifts[0, 0, 0], shifts[0, 0, 0])
+            forward_table(f_in[...], shift, perm[...], b["z"])
+            start_image(1, jnp.logical_and(step == 0, odd == 0))
+            cost_pass(which // 2 * FIRST_BLOCK, load_forward(b), True, b["g"], b["hx"], b["hy"])
 
         @pl.when(which == 1)
         def _():
             await_image(1)
             side_table(s_in[...], shifts[0, 0, 1], perm[...], b["y"])
-            cost_pass(load_side(b), False, b["g"], b["hx"], b["hy"])
-
-        coef_pass(b["hx"], b["hy"], b["wa"], b["wb"], b["a1"], b["a2"], b["i4"], b["mg"])
+            cost_pass(0, load_side(b), False, b["g"], b["hx"], b["hy"])
+
+        @pl.when(which < 2)
+        def _():
+            coef_pass(0, b["hx"], b["hy"], b["wa"], b["wb"], b["a1"], b["a2"], b["i4"], b["mg"])
+
+        @pl.when(which == 2)
+        def _():
+            coef_pass(SENT * rows, b["hx"], b["hy"], b["wa"], b["wb"], b["a1"], b["a2"], b["i4"], b["mg"])
+
+        @pl.when(jnp.logical_and(step == 0, odd == 1))
+        def _():
+            await_image(0)
+
+            @pl.when(gives_back)
+            def _():
+                for copy in back_copies:
+                    copy.start()
+
+        base = 4 * which - 6 * (which // 2)
 
         def piece_of(piece, inner):
             start = pl.multiple_of(piece * rows, rows)
@@ -425,39 +466,49 @@
             softmax_pass(start, rows, b["sc"], b["d"], b["c"])
             both = gathered(start, rows, (b["d"], b["c"]), b["back"][...])
             span = pl.ds(start, rows)
-            out_ref[4 * which, span, :] = both[:rows]
-            out_ref[4 * which + 1, span, :] = both[rows:]
-            for k, (axis, _, _) in enumerate(plan):
-                at, count = axes[axis]
-                pl.when(jnp.logical_and(which == k, at < count - 1))(piece_copy(k, piece).start)
+            out_ref[base, span, :] = both[:rows]
+            out_ref[base + 1, span, :] = both[rows:]
+            wanted = jnp.logical_or(odd == 0, jnp.logical_and(gives_back, piece < SENT))
+            pl.when(jnp.logical_and(which == 0, wanted))(piece_copy(0, piece).start)
+            at, count = axes["strip"]
+            pl.when(jnp.logical_and(which == 1, at < count - 1))(piece_copy(1, piece).start)
             return inner
 
-        lax.fori_loop(0, PIECES, piece_of, 0)
+        lax.fori_loop(which // 2 * SENT, PIECES, piece_of, 0)
+
+    def turn(step, carry):
+        pl.when(jnp.logical_or(step < 2, gets_back))(lambda: pair(step))
         return carry
 
-    lax.fori_loop(0, 2, pair, 0)
+    lax.fori_loop(0, 3, turn, 0)
 
     for which, (axis, _, _) in enumerate(plan):
         at, count = axes[axis]
         pl.when(at > 0)(image_copies[which].wait_send)
         for piece in range(PIECES):
+            near = which == 0 and piece >= SENT
+            gives, gets = (odd == 0, odd == 1) if near else (at < count - 1, at > 0)
             copy = piece_copy(which, piece)
-            pl.when(at < count - 1)(copy.wait_send)
-            pl.when(at > 0)(copy.wait_recv)
+            pl.when(gives)(copy.wait_send)
+            pl.when(gets)(copy.wait_recv)
+    for copy in back_copies:
+        pl.when(gives_back)(copy.wait_send)
 
 
 def per_device(images, offsets):
-    slots = 2 + 2 * PIECES
+    slots = 4 + 2 * PIECES
     return pl.pallas_call(
         kernel,
         out_shape=jax.ShapeDtypeStruct((8, ROWS, COLS), F32),
         in_specs=[pl.BlockSpec(memory_space=pltpu.HBM), pl.BlockSpec(memory_space=pltpu.HBM)],
         out_specs=pl.BlockSpec(memory_space=pltpu.VMEM),
         scratch_shapes=[pltpu.VMEM(*v) for v in SCRATCH.values()]
-        + [pltpu.VMEM((ROWS, COLS), F32)] * 3
+        + [pltpu.VMEM((ROWS, COLS), F32)] * 4
         + [
+            pltpu.VMEM((1, 1, 2), jnp.int32),
             pltpu.SMEM((1, 1, 2), jnp.int32),
-            pltpu.SemaphoreType.DMA((2,)),
+            pltpu.SMEM((1, 1, 2), jnp.int32),
+            pltpu.SemaphoreType.DMA((3,)),
             pltpu.SemaphoreType.DMA((slots,)),
             pltpu.SemaphoreType.DMA((slots,)),
         ],

time: 23.1 us -> 21.6 us (0.935)
  the two profiles are of different devices: /device:TPU:102 before, /device:TPU:108 now
where the time goes in v4:
time: 21.6 us; the launch traced here: 21.5 us
  Pallas kernels  20.5 us (95%)
  local copies, waits for them, and re-layouts  0.97 us (4%)
    pallas_call x1, Pallas kernels, per_device(): pl.pallas_call(kernel, out_shape=jax.ShapeDtypeStruct((8, ROWS, COLS), F3...  20.5 us
    unnamed x1, local copies, waits for them, and re-layouts  0.97 us

profile of v4, /device:TPU:108, one launch (start us, length us, event | category | flops | bytes accessed | tf_op | source)
XLA Modules:
  0.0 21.5 jit_solution(7498624690011056041)
XLA Ops:
  0.0 20.5 %shard_map.28 = f32[8,64,512]{2,1,0:T(8,128)S(1)} custom-call(s32[1,1,2]{2,1,0:T(1,128)} %offsets_ref.1, f32[64,512]{1,0:T(8,128)} %images_ref.1), custom_call_target="tpu_custom_call" | custom-call | tf_op jit(solution)/shard_map/pallas_call | solution.py:500
  20.6 1.0 %copy.4 = f32[8,64,512]{2,1,0:T(8,128)} copy(f32[8,64,512]{2,1,0:T(8,128)S(1)} %shard_map.28) | data formatting | bytes 2097152

commit v5 on v4

--- a/solution.py
+++ b/solution.py
@@ -76,7 +76,7 @@
     return out
 
 
-def guide_fields(g, perm, pad_ref, g_ref, a1_ref, a2_ref, i4_ref, mg_ref, inv_ref, then):
+def guide_fields(g, perm, pad_ref, g_ref, a1_ref, a2_ref, i4_ref, mg_ref, inv_ref, then, tile_from=0):
     gd = spread(g, perm)
     for j, v in enumerate(widened(gd)):
         g_ref[j] = v
@@ -118,7 +118,7 @@
             inv_ref[j, here, :] = inv
         return carry
 
-    lax.fori_loop(0, ROWS // SUB, tile, 0)
+    lax.fori_loop(tile_from, ROWS // SUB, tile, 0)
 
 
 def ends(shape):
@@ -390,11 +390,11 @@
         pl.when(at < count - 1)(image_copies[which].wait_recv)
 
     odd = lax.rem(axes["along"][0], 2)
-    start_image(0, odd == 1)
+    start_image(0)
     start_image(1, odd == 1)
     load_own.wait()
     load_shifts.wait()
-    guide_fields(own[...], perm[...], b["pad"], b["g"], b["a1"], b["a2"], b["i4"], b["mg"], b["inv"], lambda: start_image(0, odd == 0))
+    guide_fields(own[...], perm[...], b["pad"], b["g"], b["a1"], b["a2"], b["i4"], b["mg"], b["inv"], lambda: None)
     rows = ROWS // PIECES
     along, alongs = axes["along"]
     gives_back = jnp.logical_and(odd == 1, along < alongs - 1)
@@ -426,7 +426,7 @@
             local.start()
             f_in[...] = own[...]
             local.wait()
-            guide_fields(b_in[...], perm[...], b["pad"], b["g"], b["a1"], b["a2"], b["i4"], b["mg"], b["inv"], lambda: None)
+            guide_fields(b_in[...], perm[...], b["pad"], b["g"], b["a1"], b["a2"], b["i4"], b["mg"], b["inv"], lambda: None, max(SENT * rows // SUB - 1, 0))
 
         @pl.when(which != 1)
         def _():

time: 21.6 us -> 21.3 us (0.986)
  Pallas kernels: 20.5 us -> 20.1 us
    pallas_call x1, Pallas kernels: 20.5 us -> 20.1 us  [per_device(): pl.pallas_call(kernel, out_shape=jax.ShapeDtypeStruct((8, ROWS, COLS), F3...]
where the time goes in v5:
time: 21.3 us; the launch traced here: 21.1 us
  Pallas kernels  20.1 us (94%)
  local copies, waits for them, and re-layouts  0.97 us (5%)
    pallas_call x1, Pallas kernels, per_device(): pl.pallas_call(kernel, out_shape=jax.ShapeDtypeStruct((8, ROWS, COLS), F3...  20.1 us
    unnamed x1, local copies, waits for them, and re-layouts  0.97 us

profile of v5, /device:TPU:108, one launch (start us, length us, event | category | flops | bytes accessed | tf_op | source)
XLA Modules:
  0.0 21.1 jit_solution(11826164653692660241)
XLA Ops:
  0.0 20.1 %shard_map.28 = f32[8,64,512]{2,1,0:T(8,128)S(1)} custom-call(s32[1,1,2]{2,1,0:T(1,128)} %offsets_ref.1, f32[64,512]{1,0:T(8,128)} %images_ref.1), custom_call_target="tpu_custom_call" | custom-call | tf_op jit(solution)/shard_map/pallas_call | solution.py:500
  20.1 1.0 %copy.4 = f32[8,64,512]{2,1,0:T(8,128)} copy(f32[8,64,512]{2,1,0:T(8,128)S(1)} %shard_map.28) | data formatting | bytes 2097152
